TPU v7x, 256 devices: a whole 4x4x8 slice. The times are simulated.
256 devices in a mesh: gen: 8 (over y, core), bus: 32 (over x, z).
Axes of the slice: x: 4, y: 4, z: 8, core: 2. Of those that a mesh axis runs over, the one named last changes fastest.
Arguments:
- bus_price: float32 [32, 12, 16384], P(None, None, 'bus'), may hold values from -4 to 4
- bus_demand: float32 [32, 12, 16384], P('gen', None, 'bus'), may hold values from 0 to 2
- multipliers: float32 [2, 32, 12, 24576], P(None, 'gen', None, 'bus'), may hold values from 0 to 1
- line_limits: float32 [24576], P('bus'), may hold values from 0.3 to 3
- ptdf_blocks: bfloat16 [192, 16, 128, 128], P('bus'), may hold values from -0.125 to 0.125
- ptdf_pattern: int32 [192, 16], P('bus'), may hold values from 0 to 127, as said below
- gen_bus: int32 [4096], P(('gen', 'bus')), may hold values from 0 to 16383, as said below
- state_counts: int32 [4096], P(('gen', 'bus')), may hold values from 64 to 512, as said below
- transitions: int32 [4096, 3, 512], P(('gen', 'bus')), may hold values from 0 to 511, as said below
- state_level: float32 [4096, 512], P(('gen', 'bus')), may hold values from 0 to 3
- state_cost: float32 [4096, 512], P(('gen', 'bus')), may hold values from 0 to 2
Outputs:
- new_multipliers: float32 [2, 32, 12, 24576], P(None, 'gen', None, 'bus')
- new_price: float32 [32, 12, 16384], P(None, None, 'bus')
Inputs may be any that keep to these rules, and one draw needn't show every extreme that they name: Generator i sits in bus block (i // 16) % 32: gen_bus[i] // 512 equals that number. `state_counts`: among the generators of each aligned group of 16, at most 6 have a count above 256, and some group has exactly 6. `transitions`: every successor of a state below its generator's count is below that count; a state at or above the count has itself as every successor. `ptdf_pattern`: the 16 bus blocks named in one row are different.
All inputs are finite; a program needn't handle non-finite values.
Results may differ from a plain program's by a relative error of at most 0.0031.
Values may be sent and summed in bfloat16 or wider, within the bound.
A program may use at most 128 MiB of HBM per device.

v0:
```python
import jax
import jax.numpy as jnp
from jax import lax
from jax.sharding import PartitionSpec as P

STATES = 512
BLK = 128
NNZB = 16
HIGHEST_PRECISION = lax.Precision.HIGHEST
STEP_SIZE = 1.0


def successor_matrix(trans_rows, state_span):
    columns = jnp.arange(state_span, dtype=jnp.int32)
    operator_table = jnp.zeros((trans_rows.shape[0], state_span, state_span), jnp.bfloat16)
    for branch in range(trans_rows.shape[1]):
        operator_table = operator_table + (
            trans_rows[:, branch, :state_span, None] == columns[None, None, :]
        ).astype(jnp.bfloat16)
    return operator_table


def smoothed_plan(level_rows, cost_rows, valid_rows, operator_table, hourly_prices):
    weights = valid_rows[None, :, None, :] * jnp.exp(
        hourly_prices[..., None] * level_rows[None, :, None, :] - cost_rows[None, :, None, :]
    )
    opening = weights[0] / jnp.sum(weights[0], axis=-1, keepdims=True)

    def forward(state_now, present_weight):
        pushed = jnp.einsum(
            "hkj,hjf->hkf",
            state_now.astype(jnp.bfloat16),
            operator_table,
            preferred_element_type=jnp.float32,
        )
        raised = pushed * present_weight
        scale_now = jnp.sum(raised, axis=-1, keepdims=True)
        state_next = raised / scale_now
        return (state_next, (state_next, scale_now))

    unused_state, (states_later, scales) = lax.scan(forward, opening, weights[1:])
    states_all = jnp.concatenate([opening[None], states_later], axis=0)

    def backward(back_now, inputs):
        present_weight, scale_now = inputs
        fetched_entries = (present_weight * back_now / scale_now).astype(jnp.bfloat16)
        back_prev = jnp.einsum(
            "fjc,fhc->fjh", fetched_entries, operator_table, preferred_element_type=jnp.float32
        )
        return (back_prev, back_prev)

    ones_back = jnp.ones_like(opening)
    unused_back, backs_earlier = lax.scan(backward, ones_back, (weights[1:], scales), reverse=True)
    backs_all = jnp.concatenate([backs_earlier, ones_back[None]], axis=0)
    combined_probability = states_all * backs_all
    return jnp.sum(combined_probability * level_rows[None, :, None, :], axis=-1) / jnp.sum(
        combined_probability, axis=-1
    )


def shards(
    bus_price,
    bus_demand,
    multipliers,
    line_limits,
    ptdf_blocks,
    ptdf_pattern,
    gen_bus,
    state_counts,
    transitions,
    state_level,
    state_cost,
):
    scn_all, hour_count, bus_dev = bus_price.shape
    scn_dev = bus_demand.shape[0]
    gen_index = lax.axis_index("gen")
    bus_index = lax.axis_index("bus")
    block_total = lax.axis_size("bus") * bus_dev // BLK
    local_bus = gen_bus - bus_index * bus_dev
    onehot_all = (local_bus[:, None] == jnp.arange(bus_dev, dtype=jnp.int32)[None, :]).astype(
        jnp.float32
    )
    valid_all = (jnp.arange(STATES, dtype=jnp.int32)[None, :] < state_counts[:, None]).astype(
        jnp.float32
    )
    operator_table = successor_matrix(transitions, STATES)
    hourly_prices = jnp.einsum("rtb,gb->tgr", bus_price, onehot_all, precision=HIGHEST_PRECISION)
    output = smoothed_plan(state_level, state_cost, valid_all, operator_table, hourly_prices)
    summed = jnp.einsum("tgr,gb->rtb", output, onehot_all, precision=HIGHEST_PRECISION)
    injections = lax.psum_scatter(summed, "gen", scatter_dimension=0, tiled=True)
    row_total = scn_dev * hour_count
    network_row_block = (injections - bus_demand).astype(jnp.bfloat16).reshape(row_total, bus_dev)
    line_blocks = ptdf_blocks.shape[0]
    wanted = ptdf_pattern.reshape(-1)
    piece_cols = lax.all_gather(network_row_block, "bus", axis=1, tiled=True)
    block_count = piece_cols.shape[1] // BLK
    block_ids = jnp.arange(block_count, dtype=jnp.int32)
    chooser = (wanted[:, None] == block_ids[None, :]).astype(jnp.bfloat16)
    blocked = piece_cols.reshape(piece_cols.shape[0], block_count, BLK)
    picked_blocks = jnp.einsum("rjb,mj->rmb", blocked, chooser, preferred_element_type=jnp.float32)
    gathered = picked_blocks.astype(jnp.bfloat16).reshape(row_total, line_blocks, NNZB, BLK)
    flows = jnp.einsum("rlkb,lkbc->rlc", gathered, ptdf_blocks, preferred_element_type=jnp.float32)
    flow_lines = flows.reshape(scn_dev, hour_count, line_blocks * BLK)
    upper_old = multipliers[0]
    lower_old = multipliers[1]
    upper_new = jnp.maximum(0.0, upper_old + STEP_SIZE * (flow_lines - line_limits[None, None, :]))
    lower_new = jnp.maximum(0.0, lower_old + STEP_SIZE * (-flow_lines - line_limits[None, None, :]))
    change = (
        (upper_new - upper_old - (lower_new - lower_old))
        .astype(jnp.bfloat16)
        .reshape(row_total, line_blocks, BLK)
    )
    spread = jnp.einsum("rlc,lkbc->rlkb", change, ptdf_blocks, preferred_element_type=jnp.float32)
    placing = (
        ptdf_pattern[:, :, None] == jnp.arange(block_total, dtype=jnp.int32)[None, None, :]
    ).astype(jnp.float32)
    partial_change = jnp.einsum(
        "rlkb,lkj->rjb", spread, placing, precision=HIGHEST_PRECISION
    ).reshape(scn_dev, hour_count, block_total * BLK)
    own_change = lax.psum_scatter(partial_change, "bus", scatter_dimension=2, tiled=True)
    own_price = lax.dynamic_slice_in_dim(bus_price, gen_index * scn_dev, scn_dev, 0)
    new_share = own_price - own_change
    new_price = lax.all_gather(new_share, "gen", axis=0, tiled=True)
    return (jnp.stack([upper_new, lower_new]), new_price)


def solution(mesh):
    in_specs = (
        P(None, None, "bus"),
        P("gen", None, "bus"),
        P(None, "gen", None, "bus"),
        P("bus"),
        P("bus", None, None, None),
        P("bus", None),
        P(("gen", "bus")),
        P(("gen", "bus")),
        P(("gen", "bus"), None, None),
        P(("gen", "bus"), None),
        P(("gen", "bus"), None),
    )
    out_specs = (P(None, "gen", None, "bus"), P(None, None, "bus"))
    return jax.shard_map(shards, mesh=mesh, in_specs=in_specs, out_specs=out_specs, check_vma=False)
```

profile of v0, /device:TPU:1, one launch (start us, length us, event | category | flops | bytes accessed | tf_op | source)
XLA Modules:
  0.0 687.4 jit_solution(12709552428947251052)
XLA Ops:
  8.8 2.0 convolution_bitcast_fusion.2
  10.8 3.3 exponential_multiply_fusion
  15.4 3.4 copy-done.1
  19.9 11.2 %slice.31 = f32[11,16,32,512]{3,2,1,0:T(8,128)} slice(f32[12,16,32,512]{3,2,1,0:T(8,128)} %copy-done.1), slice={[1:12], [0:16], [0:32], [0:512]} | slice | bytes 23068672 | tf_op jit(solution)/shard_map/slice | solution.py:41
  31.1 5.7 broadcast.49.clone
  36.8 103.0 %while.32 = (s32[]{:T(128)}, bf16[16,32,512]{2,1,0:T(8,128)(2,1)}, f32[11,16,32,512]{3,2,1,0:T(8,128)}, f32[11,16,32,1]{2,1,3,0:T(8,128)S(1)}, f32[11,16,32,512]...) while((s32[]{:T(128)}, bf16[16,32,512]{2,1,0:T(8,128)(2,1)}, ...), condition=%wide.region_3.4_spmd.clone, body=%wide.region_1.3_spmd.clone.sunk | while | flops 319815168 | bytes 5361777 | solution.py:41
  36.8 8.0 %fusion.75 = (f32[16,32]{1,0:T(8,128)S(1)}, f32[16,32,512]{2,1,0:T(8,128)S(1)}) fusion(f32[11,16,32,512]{3,2,1,0:T(8,128)} %get-tuple-element.389, s32[]{:T(128)S(6)} %copy.77, s32[16,512]{1,0:T(8,128)S(1)} %get-tuple-element.392, s32[16,512]{1,0:T(8,128)S(1)} %get-tuple-element.391, s32[16,512]{1,0:T(8,128)S(1)} %get-tuple-element.390, ...), kind=kOutput, calls=%fused_computation.83.clone.1 | convolution fusion | flops 319290880 | bytes 2721796 | tf_op jit(solution)/shard_map/while/body/eval_jaxpr/hkj,hjf->hkf/dot_general | solution.py:30
  46.2 8.0 %fusion.75 = (f32[16,32]{1,0:T(8,128)S(1)}, f32[16,32,512]{2,1,0:T(8,128)S(1)}) fusion(f32[11,16,32,512]{3,2,1,0:T(8,128)} %get-tuple-element.389, s32[]{:T(128)S(6)} %copy.77, s32[16,512]{1,0:T(8,128)S(1)} %get-tuple-element.392, s32[16,512]{1,0:T(8,128)S(1)} %get-tuple-element.391, s32[16,512]{1,0:T(8,128)S(1)} %get-tuple-element.390, ...), kind=kOutput, calls=%fused_computation.83.clone.1 | convolution fusion | flops 319290880 | bytes 2721796 | tf_op jit(solution)/shard_map/while/body/eval_jaxpr/hkj,hjf->hkf/dot_general | solution.py:30
  54.2 1.3 bitcast_dynamic-update-slice_fusion.6
  55.5 8.0 %fusion.75 = (f32[16,32]{1,0:T(8,128)S(1)}, f32[16,32,512]{2,1,0:T(8,128)S(1)}) fusion(f32[11,16,32,512]{3,2,1,0:T(8,128)} %get-tuple-element.389, s32[]{:T(128)S(6)} %copy.77, s32[16,512]{1,0:T(8,128)S(1)} %get-tuple-element.392, s32[16,512]{1,0:T(8,128)S(1)} %get-tuple-element.391, s32[16,512]{1,0:T(8,128)S(1)} %get-tuple-element.390, ...), kind=kOutput, calls=%fused_computation.83.clone.1 | convolution fusion | flops 319290880 | bytes 2721796 | tf_op jit(solution)/shard_map/while/body/eval_jaxpr/hkj,hjf->hkf/dot_general | solution.py:30
  63.6 1.3 bitcast_dynamic-update-slice_fusion.6
  64.9 8.0 %fusion.75 = (f32[16,32]{1,0:T(8,128)S(1)}, f32[16,32,512]{2,1,0:T(8,128)S(1)}) fusion(f32[11,16,32,512]{3,2,1,0:T(8,128)} %get-tuple-element.389, s32[]{:T(128)S(6)} %copy.77, s32[16,512]{1,0:T(8,128)S(1)} %get-tuple-element.392, s32[16,512]{1,0:T(8,128)S(1)} %get-tuple-element.391, s32[16,512]{1,0:T(8,128)S(1)} %get-tuple-element.390, ...), kind=kOutput, calls=%fused_computation.83.clone.1 | convolution fusion | flops 319290880 | bytes 2721796 | tf_op jit(solution)/shard_map/while/body/eval_jaxpr/hkj,hjf->hkf/dot_general | solution.py:30
  72.9 1.3 bitcast_dynamic-update-slice_fusion.6
  74.3 8.0 %fusion.75 = (f32[16,32]{1,0:T(8,128)S(1)}, f32[16,32,512]{2,1,0:T(8,128)S(1)}) fusion(f32[11,16,32,512]{3,2,1,0:T(8,128)} %get-tuple-element.389, s32[]{:T(128)S(6)} %copy.77, s32[16,512]{1,0:T(8,128)S(1)} %get-tuple-element.392, s32[16,512]{1,0:T(8,128)S(1)} %get-tuple-element.391, s32[16,512]{1,0:T(8,128)S(1)} %get-tuple-element.390, ...), kind=kOutput, calls=%fused_computation.83.clone.1 | convolution fusion | flops 319290880 | bytes 2721796 | tf_op jit(solution)/shard_map/while/body/eval_jaxpr/hkj,hjf->hkf/dot_general | solution.py:30
  82.3 1.3 bitcast_dynamic-update-slice_fusion.6
  83.6 8.0 %fusion.75 = (f32[16,32]{1,0:T(8,128)S(1)}, f32[16,32,512]{2,1,0:T(8,128)S(1)}) fusion(f32[11,16,32,512]{3,2,1,0:T(8,128)} %get-tuple-element.389, s32[]{:T(128)S(6)} %copy.77, s32[16,512]{1,0:T(8,128)S(1)} %get-tuple-element.392, s32[16,512]{1,0:T(8,128)S(1)} %get-tuple-element.391, s32[16,512]{1,0:T(8,128)S(1)} %get-tuple-element.390, ...), kind=kOutput, calls=%fused_computation.83.clone.1 | convolution fusion | flops 319290880 | bytes 2721796 | tf_op jit(solution)/shard_map/while/body/eval_jaxpr/hkj,hjf->hkf/dot_general | solution.py:30
  93.0 8.0 %fusion.75 = (f32[16,32]{1,0:T(8,128)S(1)}, f32[16,32,512]{2,1,0:T(8,128)S(1)}) fusion(f32[11,16,32,512]{3,2,1,0:T(8,128)} %get-tuple-element.389, s32[]{:T(128)S(6)} %copy.77, s32[16,512]{1,0:T(8,128)S(1)} %get-tuple-element.392, s32[16,512]{1,0:T(8,128)S(1)} %get-tuple-element.391, s32[16,512]{1,0:T(8,128)S(1)} %get-tuple-element.390, ...), kind=kOutput, calls=%fused_computation.83.clone.1 | convolution fusion | flops 319290880 | bytes 2721796 | tf_op jit(solution)/shard_map/while/body/eval_jaxpr/hkj,hjf->hkf/dot_general | solution.py:30
  102.4 8.0 %fusion.75 = (f32[16,32]{1,0:T(8,128)S(1)}, f32[16,32,512]{2,1,0:T(8,128)S(1)}) fusion(f32[11,16,32,512]{3,2,1,0:T(8,128)} %get-tuple-element.389, s32[]{:T(128)S(6)} %copy.77, s32[16,512]{1,0:T(8,128)S(1)} %get-tuple-element.392, s32[16,512]{1,0:T(8,128)S(1)} %get-tuple-element.391, s32[16,512]{1,0:T(8,128)S(1)} %get-tuple-element.390, ...), kind=kOutput, calls=%fused_computation.83.clone.1 | convolution fusion | flops 319290880 | bytes 2721796 | tf_op jit(solution)/shard_map/while/body/eval_jaxpr/hkj,hjf->hkf/dot_general | solution.py:30
  111.7 8.0 %fusion.75 = (f32[16,32]{1,0:T(8,128)S(1)}, f32[16,32,512]{2,1,0:T(8,128)S(1)}) fusion(f32[11,16,32,512]{3,2,1,0:T(8,128)} %get-tuple-element.389, s32[]{:T(128)S(6)} %copy.77, s32[16,512]{1,0:T(8,128)S(1)} %get-tuple-element.392, s32[16,512]{1,0:T(8,128)S(1)} %get-tuple-element.391, s32[16,512]{1,0:T(8,128)S(1)} %get-tuple-element.390, ...), kind=kOutput, calls=%fused_computation.83.clone.1 | convolution fusion | flops 319290880 | bytes 2721796 | tf_op jit(solution)/shard_map/while/body/eval_jaxpr/hkj,hjf->hkf/dot_general | solution.py:30
  121.1 8.0 %fusion.75 = (f32[16,32]{1,0:T(8,128)S(1)}, f32[16,32,512]{2,1,0:T(8,128)S(1)}) fusion(f32[11,16,32,512]{3,2,1,0:T(8,128)} %get-tuple-element.389, s32[]{:T(128)S(6)} %copy.77, s32[16,512]{1,0:T(8,128)S(1)} %get-tuple-element.392, s32[16,512]{1,0:T(8,128)S(1)} %get-tuple-element.391, s32[16,512]{1,0:T(8,128)S(1)} %get-tuple-element.390, ...), kind=kOutput, calls=%fused_computation.83.clone.1 | convolution fusion | flops 319290880 | bytes 2721796 | tf_op jit(solution)/shard_map/while/body/eval_jaxpr/hkj,hjf->hkf/dot_general | solution.py:30
  130.4 8.0 %fusion.75 = (f32[16,32]{1,0:T(8,128)S(1)}, f32[16,32,512]{2,1,0:T(8,128)S(1)}) fusion(f32[11,16,32,512]{3,2,1,0:T(8,128)} %get-tuple-element.389, s32[]{:T(128)S(6)} %copy.77, s32[16,512]{1,0:T(8,128)S(1)} %get-tuple-element.392, s32[16,512]{1,0:T(8,128)S(1)} %get-tuple-element.391, s32[16,512]{1,0:T(8,128)S(1)} %get-tuple-element.390, ...), kind=kOutput, calls=%fused_computation.83.clone.1 | convolution fusion | flops 319290880 | bytes 2721796 | tf_op jit(solution)/shard_map/while/body/eval_jaxpr/hkj,hjf->hkf/dot_general | solution.py:30
  140.9 5.8 broadcast.49
  146.8 118.3 %while.33 = (s32[]{:T(128)}, f32[16,32,512]{2,1,0:T(8,128)}, f32[11,16,32,512]{3,2,1,0:T(8,128)}, f32[11,16,32,512]{3,2,1,0:T(8,128)}, f32[11,16,32,1]{2,1,3,0:T...) while((s32[]{:T(128)}, f32[16,32,512]{2,1,0:T(8,128)}, ...), condition=%wide.region_5.6_spmd.clone, body=%wide.region_4.5_spmd.clone.sunk | while | flops 319553536 | bytes 6397045 | solution.py:53
  148.0 9.5 %bitcast_dynamic-update-slice_fusion.8 = (f32[11,16,32,512]{3,2,1,0:T(8,128)}, f32[16,32,512]{2,1,0:T(8,128)}) fusion(f32[11,16,32,512]{3,2,1,0:T(8,128)} %get-tuple-element.406, s32[]{:T(128)S(6)} %sub.131, s32[16,512]{1,0:T(8,128)S(1)} %get-tuple-element.421, s32[16,512]{1,0:T(8,128)S(1)} %get-tuple-element.420, ...), kind=kOutput, calls=%fused_computation.31.clone.1 | convolution fusion | flops 319553536 | bytes 4295680 | tf_op jit(solution)/shard_map/while/body/eval_jaxpr/fjc,fhc->fjh/dot_general | solution.py:47
  158.8 9.5 %bitcast_dynamic-update-slice_fusion.8 = (f32[11,16,32,512]{3,2,1,0:T(8,128)}, f32[16,32,512]{2,1,0:T(8,128)}) fusion(f32[11,16,32,512]{3,2,1,0:T(8,128)} %get-tuple-element.406, s32[]{:T(128)S(6)} %sub.131, s32[16,512]{1,0:T(8,128)S(1)} %get-tuple-element.421, s32[16,512]{1,0:T(8,128)S(1)} %get-tuple-element.420, ...), kind=kOutput, calls=%fused_computation.31.clone.1 | convolution fusion | flops 319553536 | bytes 4295680 | tf_op jit(solution)/shard_map/while/body/eval_jaxpr/fjc,fhc->fjh/dot_general | solution.py:47
  169.5 9.5 %bitcast_dynamic-update-slice_fusion.8 = (f32[11,16,32,512]{3,2,1,0:T(8,128)}, f32[16,32,512]{2,1,0:T(8,128)}) fusion(f32[11,16,32,512]{3,2,1,0:T(8,128)} %get-tuple-element.406, s32[]{:T(128)S(6)} %sub.131, s32[16,512]{1,0:T(8,128)S(1)} %get-tuple-element.421, s32[16,512]{1,0:T(8,128)S(1)} %get-tuple-element.420, ...), kind=kOutput, calls=%fused_computation.31.clone.1 | convolution fusion | flops 319553536 | bytes 4295680 | tf_op jit(solution)/shard_map/while/body/eval_jaxpr/fjc,fhc->fjh/dot_general | solution.py:47
  180.3 9.5 %bitcast_dynamic-update-slice_fusion.8 = (f32[11,16,32,512]{3,2,1,0:T(8,128)}, f32[16,32,512]{2,1,0:T(8,128)}) fusion(f32[11,16,32,512]{3,2,1,0:T(8,128)} %get-tuple-element.406, s32[]{:T(128)S(6)} %sub.131, s32[16,512]{1,0:T(8,128)S(1)} %get-tuple-element.421, s32[16,512]{1,0:T(8,128)S(1)} %get-tuple-element.420, ...), kind=kOutput, calls=%fused_computation.31.clone.1 | convolution fusion | flops 319553536 | bytes 4295680 | tf_op jit(solution)/shard_map/while/body/eval_jaxpr/fjc,fhc->fjh/dot_general | solution.py:47
  191.0 9.5 %bitcast_dynamic-update-slice_fusion.8 = (f32[11,16,32,512]{3,2,1,0:T(8,128)}, f32[16,32,512]{2,1,0:T(8,128)}) fusion(f32[11,16,32,512]{3,2,1,0:T(8,128)} %get-tuple-element.406, s32[]{:T(128)S(6)} %sub.131, s32[16,512]{1,0:T(8,128)S(1)} %get-tuple-element.421, s32[16,512]{1,0:T(8,128)S(1)} %get-tuple-element.420, ...), kind=kOutput, calls=%fused_computation.31.clone.1 | convolution fusion | flops 319553536 | bytes 4295680 | tf_op jit(solution)/shard_map/while/body/eval_jaxpr/fjc,fhc->fjh/dot_general | solution.py:47
  201.8 9.5 %bitcast_dynamic-update-slice_fusion.8 = (f32[11,16,32,512]{3,2,1,0:T(8,128)}, f32[16,32,512]{2,1,0:T(8,128)}) fusion(f32[11,16,32,512]{3,2,1,0:T(8,128)} %get-tuple-element.406, s32[]{:T(128)S(6)} %sub.131, s32[16,512]{1,0:T(8,128)S(1)} %get-tuple-element.421, s32[16,512]{1,0:T(8,128)S(1)} %get-tuple-element.420, ...), kind=kOutput, calls=%fused_computation.31.clone.1 | convolution fusion | flops 319553536 | bytes 4295680 | tf_op jit(solution)/shard_map/while/body/eval_jaxpr/fjc,fhc->fjh/dot_general | solution.py:47
  212.5 9.5 %bitcast_dynamic-update-slice_fusion.8 = (f32[11,16,32,512]{3,2,1,0:T(8,128)}, f32[16,32,512]{2,1,0:T(8,128)}) fusion(f32[11,16,32,512]{3,2,1,0:T(8,128)} %get-tuple-element.406, s32[]{:T(128)S(6)} %sub.131, s32[16,512]{1,0:T(8,128)S(1)} %get-tuple-element.421, s32[16,512]{1,0:T(8,128)S(1)} %get-tuple-element.420, ...), kind=kOutput, calls=%fused_computation.31.clone.1 | convolution fusion | flops 319553536 | bytes 4295680 | tf_op jit(solution)/shard_map/while/body/eval_jaxpr/fjc,fhc->fjh/dot_general | solution.py:47
  223.3 9.5 %bitcast_dynamic-update-slice_fusion.8 = (f32[11,16,32,512]{3,2,1,0:T(8,128)}, f32[16,32,512]{2,1,0:T(8,128)}) fusion(f32[11,16,32,512]{3,2,1,0:T(8,128)} %get-tuple-element.406, s32[]{:T(128)S(6)} %sub.131, s32[16,512]{1,0:T(8,128)S(1)} %get-tuple-element.421, s32[16,512]{1,0:T(8,128)S(1)} %get-tuple-element.420, ...), kind=kOutput, calls=%fused_computation.31.clone.1 | convolution fusion | flops 319553536 | bytes 4295680 | tf_op jit(solution)/shard_map/while/body/eval_jaxpr/fjc,fhc->fjh/dot_general | solution.py:47
  234.0 9.5 %bitcast_dynamic-update-slice_fusion.8 = (f32[11,16,32,512]{3,2,1,0:T(8,128)}, f32[16,32,512]{2,1,0:T(8,128)}) fusion(f32[11,16,32,512]{3,2,1,0:T(8,128)} %get-tuple-element.406, s32[]{:T(128)S(6)} %sub.131, s32[16,512]{1,0:T(8,128)S(1)} %get-tuple-element.421, s32[16,512]{1,0:T(8,128)S(1)} %get-tuple-element.420, ...), kind=kOutput, calls=%fused_computation.31.clone.1 | convolution fusion | flops 319553536 | bytes 4295680 | tf_op jit(solution)/shard_map/while/body/eval_jaxpr/fjc,fhc->fjh/dot_general | solution.py:47
  244.8 9.5 %bitcast_dynamic-update-slice_fusion.8 = (f32[11,16,32,512]{3,2,1,0:T(8,128)}, f32[16,32,512]{2,1,0:T(8,128)}) fusion(f32[11,16,32,512]{3,2,1,0:T(8,128)} %get-tuple-element.406, s32[]{:T(128)S(6)} %sub.131, s32[16,512]{1,0:T(8,128)S(1)} %get-tuple-element.421, s32[16,512]{1,0:T(8,128)S(1)} %get-tuple-element.420, ...), kind=kOutput, calls=%fused_computation.31.clone.1 | convolution fusion | flops 319553536 | bytes 4295680 | tf_op jit(solution)/shard_map/while/body/eval_jaxpr/fjc,fhc->fjh/dot_general | solution.py:47
  255.5 9.5 %bitcast_dynamic-update-slice_fusion.8 = (f32[11,16,32,512]{3,2,1,0:T(8,128)}, f32[16,32,512]{2,1,0:T(8,128)}) fusion(f32[11,16,32,512]{3,2,1,0:T(8,128)} %get-tuple-element.406, s32[]{:T(128)S(6)} %sub.131, s32[16,512]{1,0:T(8,128)S(1)} %get-tuple-element.421, s32[16,512]{1,0:T(8,128)S(1)} %get-tuple-element.420, ...), kind=kOutput, calls=%fused_computation.31.clone.1 | convolution fusion | flops 319553536 | bytes 4295680 | tf_op jit(solution)/shard_map/while/body/eval_jaxpr/fjc,fhc->fjh/dot_general | solution.py:47
  265.1 8.9 %fusion.37 = (f32[12,16,32]{2,1,0:T(8,128)S(1)}, f32[12,16,32]{2,1,0:T(8,128)S(1)}) fusion(f32[11,16,32,512]{3,2,1,0:T(8,128)} %get-tuple-element.159, f32[11,16,32,512]{3,2,1,0:T(8,128)} %get-tuple-element.157, f32[1,16,32,512]{3,2,1,0:T(8,128)} %slice_divide_fusion, f32[16,512]{1,0:T(8,128)S(1)} %copy-done.4), kind=kLoop, calls=%fused_computation.41 | loop fusion | flops 15716352 | bytes 24199168 | tf_op jit(solution)/shard_map/reduce_sum | solution.py:56
  273.9 1.4 convolution_bitcast_fusion.1
  276.7 67.6 %all-reduce.4.cloned.1.call-done = f32[32,12,512]{2,0,1:T(8,128)} async-done(((f32[32,12,512]{2,0,1:T(8,128)}), f32[32,12,512]{2,0,1:T(8,128)}) %all-reduce.4.cloned.1.call-update) | async-done | bytes 786448
  347.0 70.2 %all-gather.2.cloned.1.call-done = bf16[48,16384]{1,0:T(8,128)(2,1)} async-done(((bf16[48,512]{1,0:T(8,128)(2,1)}), bf16[48,16384]{1,0:T(8,128)(2,1)}) %all-gather.2.cloned.1.call-update) | async-done | bytes 1572880 | tf_op jit(solution)/shard_map/all_gather | solution.py:95
  417.2 1.8 copy.48
  422.0 1.9 add_maximum_fusion.1
  423.9 1.6 squeeze.27
  425.5 1.6 squeeze.26
  427.2 2.3 convolution_bitcast_fusion
  429.4 4.0 fusion.40
  433.4 3.7 reshape.84
  439.9 219.5 %reduce-scatter.3.cloned.1.call-done = f32[4,12,512]{2,1,0:T(8,128)} async-done(((f32[4,12,16384]{2,1,0:T(8,128)}), f32[4,12,512]{2,1,0:T(8,128)}) %reduce-scatter.3.cloned.1.call-update) | async-done | bytes 98320 | tf_op jit(solution)/shard_map/reduce_scatter | solution.py:120
  660.3 19.2 %all_gather.7 = f32[32,12,512]{2,1,0:T(8,128)S(1)} all-gather(f32[4,12,512]{2,1,0:T(8,128)S(1)} %copy_subtract_fusion), channel_id=1, replica_groups=mesh['gen'=8,'bus'=32] {'gen'}, dimensions={0}, use_global_device_ids=true | all-gather | bytes 884736 | tf_op jit(solution)/shard_map/all_gather | solution.py:123
  679.5 1.3 copy.39
  (85 shorter events, 38.1 us)
Async XLA Ops:
  7.2 412.3 %copy-start = (bf16[6,16,128,128]{3,2,1,0:T(8,128)(2,1)S(1)}, bf16[6,16,128,128]{3,2,1,0:T(8,128)(2,1)}, u32[]{:S(2)}) copy-start(bf16[6,16,128,128]{3,2,1,0:T(8,128)(2,1)} %param.19) | copy-start | bytes 9437188
  7.2 337.1 %all-reduce.4.cloned.1.call-start = ((), (), s32[]{:S(2)}) async-start(), calls=%async_computation.3 | async-start | bytes 1572864
  14.2 4.7 copy-start.1
  19.9 11.2 %copy-start.5 = (s32[16,3,512]{2,0,1:T(8,128)S(1)}, s32[16,3,512]{2,0,1:T(8,128)}, u32[]{:S(2)}) copy-start(s32[16,3,512]{2,0,1:T(8,128)} %param.23) | copy-start | bytes 294916
  146.8 118.3 %copy-start.4 = (f32[16,512]{1,0:T(8,128)S(1)}, f32[16,512]{1,0:T(8,128)}, u32[]{:S(2)}) copy-start(f32[16,512]{1,0:T(8,128)} %param.24) | copy-start | bytes 98308
  265.0 10.4 %copy-start.8 = (u32[256]{0:T(256)S(1)}, u32[256]{0:T(256)}, u32[]{:S(2)}) copy-start(u32[256]{0:T(256)} %constant.88) | copy-start | bytes 3076
  265.0 81.2 %copy-start.7 = (s32[6,16]{1,0:T(8,128)S(1)}, s32[6,16]{1,0:T(8,128)}, u32[]{:S(2)}) copy-start(s32[6,16]{1,0:T(8,128)} %param.20) | copy-start | bytes 1156
  265.0 81.2 %copy-start.3 = (f32[2,4,12,768]{3,1,2,0:T(4,128)S(1)}, f32[2,4,12,768]{3,1,2,0:T(4,128)}, u32[]{:S(2)}) copy-start(f32[2,4,12,768]{3,1,2,0:T(4,128)} %param.17) | copy-start | bytes 884740
  273.9 148.1 %copy-start.6 = (f32[768]{0:T(1024)S(1)}, f32[768]{0:T(1024)}, u32[]{:S(2)}) copy-start(f32[768]{0:T(1024)} %param.18) | copy-start | bytes 9220
  275.4 141.8 %all-gather.2.cloned.1.call-start = ((), (), s32[]{:S(2)}) async-start(), calls=%async_computation.1 | async-start | bytes 1622016 | tf_op jit(solution)/shard_map/all_gather | solution.py:95
  346.0 313.4 %reduce-scatter.3.cloned.1.call-start = ((), (), s32[]{:S(2)}) async-start(), calls=%async_computation.2 | async-start | bytes 4325376 | tf_op jit(solution)/shard_map/reduce_scatter | solution.py:120
  427.2 10.9 %copy-start.2 = (f32[1,4,12,768]{3,2,1,0:T(8,128)S(1)}, f32[1,4,12,768]{3,2,1,0:T(8,128)}, u32[]{:S(2)}) copy-start(f32[1,4,12,768]{3,2,1,0:T(8,128)} %get-tuple-element.248) | copy-start | bytes 442372
Sparse Core Ops, SparseCore 0:
  275.5 68.7 all-reduce.3
  347.3 69.8 all-gather.1
  437.2 222.1 reduce-scatter.2
where the time goes:
time: 692 us; the launch traced here: 687 us
  waiting for transfers between devices  357 us (52%)
  matrix products  204 us (29%)
  local copies, waits for them, and re-layouts  56.4 us (8%)
  other arithmetic  35.5 us (5%)
  blocking collectives  19.2 us (3%)
  between operations  14.6 us (2%)
    reduce_scatter x1, waiting for transfers between devices, shards(): lax.psum_scatter(partial_change, 'bus', scatter_dimension=2, tiled=True)  219 us
    dot_general x11, matrix products, backward(): jnp.einsum('fjc,fhc->fjh', fetched_entries, operator_table, preferred_ele...  105 us
    dot_general x11, matrix products, forward(): jnp.einsum('hkj,hjf->hkf', state_now.astype(jnp.bfloat16), operator_table...  88.4 us
    all_gather x1, waiting for transfers between devices, shards(): piece_cols = lax.all_gather(network_row_block, 'bus', axis=1, tiled=True)  70.2 us
    unnamed x4, waiting for transfers between devices  67.6 us
    all_gather x1, blocking collectives, shards(): new_price = lax.all_gather(new_share, 'gen', axis=0, tiled=True)  19.2 us
    dynamic_update_slice x11, other arithmetic, smoothed_plan(): lax.scan(forward, opening, weights[1:])  14.5 us
  transfers between devices with their start and end apart: 3, of which 3 were waited for; matrix products, arithmetic and copies ran while one was open for 1% of the time, Pallas kernels for 0%

commit v1 on v0

--- a/solution.py
+++ b/solution.py
@@ -92,7 +92,9 @@
     network_row_block = (injections - bus_demand).astype(jnp.bfloat16).reshape(row_total, bus_dev)
     line_blocks = ptdf_blocks.shape[0]
     wanted = ptdf_pattern.reshape(-1)
-    piece_cols = lax.all_gather(network_row_block, "bus", axis=1, tiled=True)
+    piece_cols = jnp.concatenate(
+        lax.all_to_all(jnp.stack([network_row_block] * lax.axis_size("bus")), "bus", 0, 0), axis=1
+    )
     block_count = piece_cols.shape[1] // BLK
     block_ids = jnp.arange(block_count, dtype=jnp.int32)
     chooser = (wanted[:, None] == block_ids[None, :]).astype(jnp.bfloat16)

time: 692 us -> 672 us (0.971)
  waiting for transfers between devices: 357 us -> 319 us
  starting transfers between devices: 0.3 us -> 9.91 us
    all_gather x1 -> x0, waiting for transfers between devices: 70.2 us -> none  [shards(): piece_cols = lax.all_gather(network_row_block, 'bus', axis=1, tiled=True)]
    all_to_all x0 -> x1, waiting for transfers between devices: none -> 34.4 us  [shards(): lax.all_to_all(jnp.stack([network_row_block] * lax.axis_size('bus')), 'bu...]
    all_to_all x0 -> x1, starting transfers between devices: none -> 9.65 us  [shards(): lax.all_to_all(jnp.stack([network_row_block] * lax.axis_size('bus')), 'bu...]
    another operation x2 -> x5, local copies, waits for them, and re-layouts: 11.5 us -> 16.6 us
    unnamed x4 -> x3, waiting for transfers between devices: 67.6 us -> 67.7 us
where the time goes in v1:
time: 672 us; the launch traced here: 668 us
  waiting for transfers between devices  319 us (47%)
  matrix products  206 us (31%)
  local copies, waits for them, and re-layouts  63.1 us (9%)
  other arithmetic  35.4 us (5%)
  blocking collectives  19.6 us (3%)
  between operations  14.9 us (2%)
  starting transfers between devices  9.91 us (1%)
    reduce_scatter x1, waiting for transfers between devices, shards(): lax.psum_scatter(partial_change, 'bus', scatter_dimension=2, tiled=True)  217 us
    dot_general x11, matrix products, backward(): jnp.einsum('fjc,fhc->fjh', fetched_entries, operator_table, preferred_ele...  105 us
    dot_general x11, matrix products, forward(): jnp.einsum('hkj,hjf->hkf', state_now.astype(jnp.bfloat16), operator_table...  88.4 us
    unnamed x3, waiting for transfers between devices  67.7 us
    all_to_all x1, waiting for transfers between devices, shards(): lax.all_to_all(jnp.stack([network_row_block] * lax.axis_size('bus')), 'bu...  34.4 us
    all_gather x1, blocking collectives, shards(): new_price = lax.all_gather(new_share, 'gen', axis=0, tiled=True)  19.6 us
    dynamic_update_slice x11, other arithmetic, smoothed_plan(): lax.scan(forward, opening, weights[1:])  14.5 us
    while x11, local copies, waits for them, and re-layouts  13.5 us
  transfers between devices with their start and end apart: 3, of which 3 were waited for; matrix products, arithmetic and copies ran while one was open for 1% of the time, Pallas kernels for 0%

profile of v1, /device:TPU:1, one launch (start us, length us, event | category | flops | bytes accessed | tf_op | source)
XLA Modules:
  0.0 668.1 jit_solution(3912871025889968397)
XLA Ops:
  8.8 2.0 convolution_bitcast_fusion.2
  10.8 3.3 exponential_multiply_fusion
  15.4 3.4 copy-done.1
  19.9 11.2 %slice.31 = f32[11,16,32,512]{3,2,1,0:T(8,128)} slice(f32[12,16,32,512]{3,2,1,0:T(8,128)} %copy-done.1), slice={[1:12], [0:16], [0:32], [0:512]} | slice | bytes 23068672 | tf_op jit(solution)/shard_map/slice | solution.py:41
  31.1 5.7 broadcast.50.clone
  36.8 103.0 %while.32 = (s32[]{:T(128)}, bf16[16,32,512]{2,1,0:T(8,128)(2,1)}, f32[11,16,32,512]{3,2,1,0:T(8,128)}, f32[11,16,32,1]{2,1,3,0:T(8,128)S(1)}, f32[11,16,32,512]...) while((s32[]{:T(128)}, bf16[16,32,512]{2,1,0:T(8,128)(2,1)}, ...), condition=%wide.region_3.4_spmd.clone, body=%wide.region_1.3_spmd.clone.sunk | while | flops 319815168 | bytes 5361777 | solution.py:41
  36.8 8.0 %fusion.75 = (f32[16,32]{1,0:T(8,128)S(1)}, f32[16,32,512]{2,1,0:T(8,128)S(1)}) fusion(f32[11,16,32,512]{3,2,1,0:T(8,128)} %get-tuple-element.389, s32[]{:T(128)S(6)} %copy.77, s32[16,512]{1,0:T(8,128)S(1)} %get-tuple-element.392, s32[16,512]{1,0:T(8,128)S(1)} %get-tuple-element.391, s32[16,512]{1,0:T(8,128)S(1)} %get-tuple-element.390, ...), kind=kOutput, calls=%fused_computation.83.clone.1 | convolution fusion | flops 319290880 | bytes 2721796 | tf_op jit(solution)/shard_map/while/body/eval_jaxpr/hkj,hjf->hkf/dot_general | solution.py:30
  46.1 8.0 %fusion.75 = (f32[16,32]{1,0:T(8,128)S(1)}, f32[16,32,512]{2,1,0:T(8,128)S(1)}) fusion(f32[11,16,32,512]{3,2,1,0:T(8,128)} %get-tuple-element.389, s32[]{:T(128)S(6)} %copy.77, s32[16,512]{1,0:T(8,128)S(1)} %get-tuple-element.392, s32[16,512]{1,0:T(8,128)S(1)} %get-tuple-element.391, s32[16,512]{1,0:T(8,128)S(1)} %get-tuple-element.390, ...), kind=kOutput, calls=%fused_computation.83.clone.1 | convolution fusion | flops 319290880 | bytes 2721796 | tf_op jit(solution)/shard_map/while/body/eval_jaxpr/hkj,hjf->hkf/dot_general | solution.py:30
  55.5 8.0 %fusion.75 = (f32[16,32]{1,0:T(8,128)S(1)}, f32[16,32,512]{2,1,0:T(8,128)S(1)}) fusion(f32[11,16,32,512]{3,2,1,0:T(8,128)} %get-tuple-element.389, s32[]{:T(128)S(6)} %copy.77, s32[16,512]{1,0:T(8,128)S(1)} %get-tuple-element.392, s32[16,512]{1,0:T(8,128)S(1)} %get-tuple-element.391, s32[16,512]{1,0:T(8,128)S(1)} %get-tuple-element.390, ...), kind=kOutput, calls=%fused_computation.83.clone.1 | convolution fusion | flops 319290880 | bytes 2721796 | tf_op jit(solution)/shard_map/while/body/eval_jaxpr/hkj,hjf->hkf/dot_general | solution.py:30
  64.9 8.0 %fusion.75 = (f32[16,32]{1,0:T(8,128)S(1)}, f32[16,32,512]{2,1,0:T(8,128)S(1)}) fusion(f32[11,16,32,512]{3,2,1,0:T(8,128)} %get-tuple-element.389, s32[]{:T(128)S(6)} %copy.77, s32[16,512]{1,0:T(8,128)S(1)} %get-tuple-element.392, s32[16,512]{1,0:T(8,128)S(1)} %get-tuple-element.391, s32[16,512]{1,0:T(8,128)S(1)} %get-tuple-element.390, ...), kind=kOutput, calls=%fused_computation.83.clone.1 | convolution fusion | flops 319290880 | bytes 2721796 | tf_op jit(solution)/shard_map/while/body/eval_jaxpr/hkj,hjf->hkf/dot_general | solution.py:30
  74.2 8.0 %fusion.75 = (f32[16,32]{1,0:T(8,128)S(1)}, f32[16,32,512]{2,1,0:T(8,128)S(1)}) fusion(f32[11,16,32,512]{3,2,1,0:T(8,128)} %get-tuple-element.389, s32[]{:T(128)S(6)} %copy.77, s32[16,512]{1,0:T(8,128)S(1)} %get-tuple-element.392, s32[16,512]{1,0:T(8,128)S(1)} %get-tuple-element.391, s32[16,512]{1,0:T(8,128)S(1)} %get-tuple-element.390, ...), kind=kOutput, calls=%fused_computation.83.clone.1 | convolution fusion | flops 319290880 | bytes 2721796 | tf_op jit(solution)/shard_map/while/body/eval_jaxpr/hkj,hjf->hkf/dot_general | solution.py:30
  83.6 8.0 %fusion.75 = (f32[16,32]{1,0:T(8,128)S(1)}, f32[16,32,512]{2,1,0:T(8,128)S(1)}) fusion(f32[11,16,32,512]{3,2,1,0:T(8,128)} %get-tuple-element.389, s32[]{:T(128)S(6)} %copy.77, s32[16,512]{1,0:T(8,128)S(1)} %get-tuple-element.392, s32[16,512]{1,0:T(8,128)S(1)} %get-tuple-element.391, s32[16,512]{1,0:T(8,128)S(1)} %get-tuple-element.390, ...), kind=kOutput, calls=%fused_computation.83.clone.1 | convolution fusion | flops 319290880 | bytes 2721796 | tf_op jit(solution)/shard_map/while/body/eval_jaxpr/hkj,hjf->hkf/dot_general | solution.py:30
  93.0 8.0 %fusion.75 = (f32[16,32]{1,0:T(8,128)S(1)}, f32[16,32,512]{2,1,0:T(8,128)S(1)}) fusion(f32[11,16,32,512]{3,2,1,0:T(8,128)} %get-tuple-element.389, s32[]{:T(128)S(6)} %copy.77, s32[16,512]{1,0:T(8,128)S(1)} %get-tuple-element.392, s32[16,512]{1,0:T(8,128)S(1)} %get-tuple-element.391, s32[16,512]{1,0:T(8,128)S(1)} %get-tuple-element.390, ...), kind=kOutput, calls=%fused_computation.83.clone.1 | convolution fusion | flops 319290880 | bytes 2721796 | tf_op jit(solution)/shard_map/while/body/eval_jaxpr/hkj,hjf->hkf/dot_general | solution.py:30
  102.3 8.0 %fusion.75 = (f32[16,32]{1,0:T(8,128)S(1)}, f32[16,32,512]{2,1,0:T(8,128)S(1)}) fusion(f32[11,16,32,512]{3,2,1,0:T(8,128)} %get-tuple-element.389, s32[]{:T(128)S(6)} %copy.77, s32[16,512]{1,0:T(8,128)S(1)} %get-tuple-element.392, s32[16,512]{1,0:T(8,128)S(1)} %get-tuple-element.391, s32[16,512]{1,0:T(8,128)S(1)} %get-tuple-element.390, ...), kind=kOutput, calls=%fused_computation.83.clone.1 | convolution fusion | flops 319290880 | bytes 2721796 | tf_op jit(solution)/shard_map/while/body/eval_jaxpr/hkj,hjf->hkf/dot_general | solution.py:30
  111.7 8.0 %fusion.75 = (f32[16,32]{1,0:T(8,128)S(1)}, f32[16,32,512]{2,1,0:T(8,128)S(1)}) fusion(f32[11,16,32,512]{3,2,1,0:T(8,128)} %get-tuple-element.389, s32[]{:T(128)S(6)} %copy.77, s32[16,512]{1,0:T(8,128)S(1)} %get-tuple-element.392, s32[16,512]{1,0:T(8,128)S(1)} %get-tuple-element.391, s32[16,512]{1,0:T(8,128)S(1)} %get-tuple-element.390, ...), kind=kOutput, calls=%fused_computation.83.clone.1 | convolution fusion | flops 319290880 | bytes 2721796 | tf_op jit(solution)/shard_map/while/body/eval_jaxpr/hkj,hjf->hkf/dot_general | solution.py:30
  121.1 8.0 %fusion.75 = (f32[16,32]{1,0:T(8,128)S(1)}, f32[16,32,512]{2,1,0:T(8,128)S(1)}) fusion(f32[11,16,32,512]{3,2,1,0:T(8,128)} %get-tuple-element.389, s32[]{:T(128)S(6)} %copy.77, s32[16,512]{1,0:T(8,128)S(1)} %get-tuple-element.392, s32[16,512]{1,0:T(8,128)S(1)} %get-tuple-element.391, s32[16,512]{1,0:T(8,128)S(1)} %get-tuple-element.390, ...), kind=kOutput, calls=%fused_computation.83.clone.1 | convolution fusion | flops 319290880 | bytes 2721796 | tf_op jit(solution)/shard_map/while/body/eval_jaxpr/hkj,hjf->hkf/dot_general | solution.py:30
  130.4 8.0 %fusion.75 = (f32[16,32]{1,0:T(8,128)S(1)}, f32[16,32,512]{2,1,0:T(8,128)S(1)}) fusion(f32[11,16,32,512]{3,2,1,0:T(8,128)} %get-tuple-element.389, s32[]{:T(128)S(6)} %copy.77, s32[16,512]{1,0:T(8,128)S(1)} %get-tuple-element.392, s32[16,512]{1,0:T(8,128)S(1)} %get-tuple-element.391, s32[16,512]{1,0:T(8,128)S(1)} %get-tuple-element.390, ...), kind=kOutput, calls=%fused_computation.83.clone.1 | convolution fusion | flops 319290880 | bytes 2721796 | tf_op jit(solution)/shard_map/while/body/eval_jaxpr/hkj,hjf->hkf/dot_general | solution.py:30
  140.9 5.8 broadcast.50
  146.7 118.4 %while.33 = (s32[]{:T(128)}, f32[16,32,512]{2,1,0:T(8,128)}, f32[11,16,32,512]{3,2,1,0:T(8,128)}, f32[11,16,32,512]{3,2,1,0:T(8,128)}, f32[11,16,32,1]{2,1,3,0:T...) while((s32[]{:T(128)}, f32[16,32,512]{2,1,0:T(8,128)}, ...), condition=%wide.region_5.6_spmd.clone, body=%wide.region_4.5_spmd.clone.sunk | while | flops 319553536 | bytes 6397045 | solution.py:53
  148.0 9.5 %bitcast_dynamic-update-slice_fusion.8 = (f32[11,16,32,512]{3,2,1,0:T(8,128)}, f32[16,32,512]{2,1,0:T(8,128)}) fusion(f32[11,16,32,512]{3,2,1,0:T(8,128)} %get-tuple-element.406, s32[]{:T(128)S(6)} %sub.131, s32[16,512]{1,0:T(8,128)S(1)} %get-tuple-element.421, s32[16,512]{1,0:T(8,128)S(1)} %get-tuple-element.420, ...), kind=kOutput, calls=%fused_computation.31.clone.1 | convolution fusion | flops 319553536 | bytes 4295680 | tf_op jit(solution)/shard_map/while/body/eval_jaxpr/fjc,fhc->fjh/dot_general | solution.py:47
  158.7 9.5 %bitcast_dynamic-update-slice_fusion.8 = (f32[11,16,32,512]{3,2,1,0:T(8,128)}, f32[16,32,512]{2,1,0:T(8,128)}) fusion(f32[11,16,32,512]{3,2,1,0:T(8,128)} %get-tuple-element.406, s32[]{:T(128)S(6)} %sub.131, s32[16,512]{1,0:T(8,128)S(1)} %get-tuple-element.421, s32[16,512]{1,0:T(8,128)S(1)} %get-tuple-element.420, ...), kind=kOutput, calls=%fused_computation.31.clone.1 | convolution fusion | flops 319553536 | bytes 4295680 | tf_op jit(solution)/shard_map/while/body/eval_jaxpr/fjc,fhc->fjh/dot_general | solution.py:47
  169.5 9.5 %bitcast_dynamic-update-slice_fusion.8 = (f32[11,16,32,512]{3,2,1,0:T(8,128)}, f32[16,32,512]{2,1,0:T(8,128)}) fusion(f32[11,16,32,512]{3,2,1,0:T(8,128)} %get-tuple-element.406, s32[]{:T(128)S(6)} %sub.131, s32[16,512]{1,0:T(8,128)S(1)} %get-tuple-element.421, s32[16,512]{1,0:T(8,128)S(1)} %get-tuple-element.420, ...), kind=kOutput, calls=%fused_computation.31.clone.1 | convolution fusion | flops 319553536 | bytes 4295680 | tf_op jit(solution)/shard_map/while/body/eval_jaxpr/fjc,fhc->fjh/dot_general | solution.py:47
  180.3 9.5 %bitcast_dynamic-update-slice_fusion.8 = (f32[11,16,32,512]{3,2,1,0:T(8,128)}, f32[16,32,512]{2,1,0:T(8,128)}) fusion(f32[11,16,32,512]{3,2,1,0:T(8,128)} %get-tuple-element.406, s32[]{:T(128)S(6)} %sub.131, s32[16,512]{1,0:T(8,128)S(1)} %get-tuple-element.421, s32[16,512]{1,0:T(8,128)S(1)} %get-tuple-element.420, ...), kind=kOutput, calls=%fused_computation.31.clone.1 | convolution fusion | flops 319553536 | bytes 4295680 | tf_op jit(solution)/shard_map/while/body/eval_jaxpr/fjc,fhc->fjh/dot_general | solution.py:47
  191.0 9.6 %bitcast_dynamic-update-slice_fusion.8 = (f32[11,16,32,512]{3,2,1,0:T(8,128)}, f32[16,32,512]{2,1,0:T(8,128)}) fusion(f32[11,16,32,512]{3,2,1,0:T(8,128)} %get-tuple-element.406, s32[]{:T(128)S(6)} %sub.131, s32[16,512]{1,0:T(8,128)S(1)} %get-tuple-element.421, s32[16,512]{1,0:T(8,128)S(1)} %get-tuple-element.420, ...), kind=kOutput, calls=%fused_computation.31.clone.1 | convolution fusion | flops 319553536 | bytes 4295680 | tf_op jit(solution)/shard_map/while/body/eval_jaxpr/fjc,fhc->fjh/dot_general | solution.py:47
  201.8 9.5 %bitcast_dynamic-update-slice_fusion.8 = (f32[11,16,32,512]{3,2,1,0:T(8,128)}, f32[16,32,512]{2,1,0:T(8,128)}) fusion(f32[11,16,32,512]{3,2,1,0:T(8,128)} %get-tuple-element.406, s32[]{:T(128)S(6)} %sub.131, s32[16,512]{1,0:T(8,128)S(1)} %get-tuple-element.421, s32[16,512]{1,0:T(8,128)S(1)} %get-tuple-element.420, ...), kind=kOutput, calls=%fused_computation.31.clone.1 | convolution fusion | flops 319553536 | bytes 4295680 | tf_op jit(solution)/shard_map/while/body/eval_jaxpr/fjc,fhc->fjh/dot_general | solution.py:47
  212.6 9.5 %bitcast_dynamic-update-slice_fusion.8 = (f32[11,16,32,512]{3,2,1,0:T(8,128)}, f32[16,32,512]{2,1,0:T(8,128)}) fusion(f32[11,16,32,512]{3,2,1,0:T(8,128)} %get-tuple-element.406, s32[]{:T(128)S(6)} %sub.131, s32[16,512]{1,0:T(8,128)S(1)} %get-tuple-element.421, s32[16,512]{1,0:T(8,128)S(1)} %get-tuple-element.420, ...), kind=kOutput, calls=%fused_computation.31.clone.1 | convolution fusion | flops 319553536 | bytes 4295680 | tf_op jit(solution)/shard_map/while/body/eval_jaxpr/fjc,fhc->fjh/dot_general | solution.py:47
  223.4 9.5 %bitcast_dynamic-update-slice_fusion.8 = (f32[11,16,32,512]{3,2,1,0:T(8,128)}, f32[16,32,512]{2,1,0:T(8,128)}) fusion(f32[11,16,32,512]{3,2,1,0:T(8,128)} %get-tuple-element.406, s32[]{:T(128)S(6)} %sub.131, s32[16,512]{1,0:T(8,128)S(1)} %get-tuple-element.421, s32[16,512]{1,0:T(8,128)S(1)} %get-tuple-element.420, ...), kind=kOutput, calls=%fused_computation.31.clone.1 | convolution fusion | flops 319553536 | bytes 4295680 | tf_op jit(solution)/shard_map/while/body/eval_jaxpr/fjc,fhc->fjh/dot_general | solution.py:47
  234.1 9.5 %bitcast_dynamic-update-slice_fusion.8 = (f32[11,16,32,512]{3,2,1,0:T(8,128)}, f32[16,32,512]{2,1,0:T(8,128)}) fusion(f32[11,16,32,512]{3,2,1,0:T(8,128)} %get-tuple-element.406, s32[]{:T(128)S(6)} %sub.131, s32[16,512]{1,0:T(8,128)S(1)} %get-tuple-element.421, s32[16,512]{1,0:T(8,128)S(1)} %get-tuple-element.420, ...), kind=kOutput, calls=%fused_computation.31.clone.1 | convolution fusion | flops 319553536 | bytes 4295680 | tf_op jit(solution)/shard_map/while/body/eval_jaxpr/fjc,fhc->fjh/dot_general | solution.py:47
  244.9 9.5 %bitcast_dynamic-update-slice_fusion.8 = (f32[11,16,32,512]{3,2,1,0:T(8,128)}, f32[16,32,512]{2,1,0:T(8,128)}) fusion(f32[11,16,32,512]{3,2,1,0:T(8,128)} %get-tuple-element.406, s32[]{:T(128)S(6)} %sub.131, s32[16,512]{1,0:T(8,128)S(1)} %get-tuple-element.421, s32[16,512]{1,0:T(8,128)S(1)} %get-tuple-element.420, ...), kind=kOutput, calls=%fused_computation.31.clone.1 | convolution fusion | flops 319553536 | bytes 4295680 | tf_op jit(solution)/shard_map/while/body/eval_jaxpr/fjc,fhc->fjh/dot_general | solution.py:47
  255.6 9.5 %bitcast_dynamic-update-slice_fusion.8 = (f32[11,16,32,512]{3,2,1,0:T(8,128)}, f32[16,32,512]{2,1,0:T(8,128)}) fusion(f32[11,16,32,512]{3,2,1,0:T(8,128)} %get-tuple-element.406, s32[]{:T(128)S(6)} %sub.131, s32[16,512]{1,0:T(8,128)S(1)} %get-tuple-element.421, s32[16,512]{1,0:T(8,128)S(1)} %get-tuple-element.420, ...), kind=kOutput, calls=%fused_computation.31.clone.1 | convolution fusion | flops 319553536 | bytes 4295680 | tf_op jit(solution)/shard_map/while/body/eval_jaxpr/fjc,fhc->fjh/dot_general | solution.py:47
  265.2 8.9 %fusion.37 = (f32[12,16,32]{2,1,0:T(8,128)S(1)}, f32[12,16,32]{2,1,0:T(8,128)S(1)}) fusion(f32[11,16,32,512]{3,2,1,0:T(8,128)} %get-tuple-element.159, f32[11,16,32,512]{3,2,1,0:T(8,128)} %get-tuple-element.157, f32[1,16,32,512]{3,2,1,0:T(8,128)} %slice_divide_fusion, f32[16,512]{1,0:T(8,128)S(1)} %copy-done.4), kind=kLoop, calls=%fused_computation.41 | loop fusion | flops 15716352 | bytes 24199168 | tf_op jit(solution)/shard_map/reduce_sum | solution.py:56
  274.0 1.4 convolution_bitcast_fusion.1
  276.7 67.6 %all-reduce.4.cloned.1.call-done = f32[32,12,512]{2,0,1:T(8,128)} async-done(((f32[32,12,512]{2,0,1:T(8,128)}), f32[32,12,512]{2,0,1:T(8,128)}) %all-reduce.4.cloned.1.call-update) | async-done | bytes 786448
  345.4 1.3 stack.8
  346.8 9.7 %all-to-all-start = ((bf16[32,48,512]{2,1,0:T(8,128)(2,1)}), bf16[32,48,512]{2,1,0:T(8,128)(2,1)}, u32[]{:S(2)}, u32[]{:S(2)}) async-start(bf16[32,48,512]{2,1,0:T(8,128)(2,1)} %stack.8), calls=%async_computation | async-start | bytes 3145728 | tf_op jit(solution)/shard_map/all_to_all | solution.py:96
  358.2 34.4 %all-to-all-done = bf16[32,48,512]{2,1,0:T(8,128)(2,1)} async-done(((bf16[32,48,512]{2,1,0:T(8,128)(2,1)}), bf16[32,48,512]{2,1,0:T(8,128)(2,1)}, u32[]{:S(2)}, u32[]{:S(2)}) %all-to-all-start) | async-done | bytes 1572896 | tf_op jit(solution)/shard_map/all_to_all | solution.py:96
  392.6 3.4 copy.29
  396.0 3.8 reshape_reshape.3
  399.7 1.9 convolution_convert_fusion
  404.2 1.9 add_maximum_fusion.1
  406.1 1.6 squeeze.27
  407.7 1.6 squeeze.26
  409.3 2.3 convolution_bitcast_fusion
  411.6 4.0 fusion.40
  415.6 3.6 reshape.82
  422.1 217.3 %reduce-scatter.3.cloned.1.call-done = f32[4,12,512]{2,1,0:T(8,128)} async-done(((f32[4,12,16384]{2,1,0:T(8,128)}), f32[4,12,512]{2,1,0:T(8,128)}) %reduce-scatter.3.cloned.1.call-update) | async-done | bytes 98320 | tf_op jit(solution)/shard_map/reduce_scatter | solution.py:122
  640.3 19.6 %all_gather.3 = f32[32,12,512]{2,1,0:T(8,128)S(1)} all-gather(f32[4,12,512]{2,1,0:T(8,128)S(1)} %copy_subtract_fusion), channel_id=1, replica_groups=mesh['gen'=8,'bus'=32] {'gen'}, dimensions={0}, use_global_device_ids=true | all-gather | bytes 884736 | tf_op jit(solution)/shard_map/all_gather | solution.py:125
  659.9 1.3 copy.40
  (86 shorter events, 42.8 us)
Async XLA Ops:
  7.2 394.5 %copy-start = (bf16[6,16,128,128]{3,2,1,0:T(8,128)(2,1)S(1)}, bf16[6,16,128,128]{3,2,1,0:T(8,128)(2,1)}, u32[]{:S(2)}) copy-start(bf16[6,16,128,128]{3,2,1,0:T(8,128)(2,1)} %param.19) | copy-start | bytes 9437188
  7.2 337.2 %all-reduce.4.cloned.1.call-start = ((), (), s32[]{:S(2)}) async-start(), calls=%async_computation.3 | async-start | bytes 1572864
  14.2 4.7 copy-start.1
  19.9 11.2 %copy-start.5 = (s32[16,3,512]{2,0,1:T(8,128)S(1)}, s32[16,3,512]{2,0,1:T(8,128)}, u32[]{:S(2)}) copy-start(s32[16,3,512]{2,0,1:T(8,128)} %param.23) | copy-start | bytes 294916
  146.7 118.4 %copy-start.4 = (f32[16,512]{1,0:T(8,128)S(1)}, f32[16,512]{1,0:T(8,128)}, u32[]{:S(2)}) copy-start(f32[16,512]{1,0:T(8,128)} %param.24) | copy-start | bytes 98308
  265.2 10.3 %copy-start.8 = (u32[256]{0:T(256)S(1)}, u32[256]{0:T(256)}, u32[]{:S(2)}) copy-start(u32[256]{0:T(256)} %constant.88) | copy-start | bytes 3076
  265.2 92.3 %copy-start.3 = (f32[2,4,12,768]{3,1,2,0:T(4,128)S(1)}, f32[2,4,12,768]{3,1,2,0:T(4,128)}, u32[]{:S(2)}) copy-start(f32[2,4,12,768]{3,1,2,0:T(4,128)} %param.17) | copy-start | bytes 884740
  345.4 58.8 %copy-start.6 = (f32[768]{0:T(1024)S(1)}, f32[768]{0:T(1024)}, u32[]{:S(2)}) copy-start(f32[768]{0:T(1024)} %param.18) | copy-start | bytes 9220
  346.8 45.8 %all-to-all-start = ((bf16[32,48,512]{2,1,0:T(8,128)(2,1)}), bf16[32,48,512]{2,1,0:T(8,128)(2,1)}, u32[]{:S(2)}, u32[]{:S(2)}) async-start(bf16[32,48,512]{2,1,0:T(8,128)(2,1)} %stack.8), calls=%async_computation | async-start | bytes 3145728 | tf_op jit(solution)/shard_map/all_to_all | solution.py:96
  356.4 283.0 %reduce-scatter.3.cloned.1.call-start = ((), (), s32[]{:S(2)}) async-start(), calls=%async_computation.2 | async-start | bytes 4325376 | tf_op jit(solution)/shard_map/reduce_scatter | solution.py:122
  396.0 15.6 %copy-start.7 = (s32[6,16]{1,0:T(8,128)S(1)}, s32[6,16]{1,0:T(8,128)}, u32[]{:S(2)}) copy-start(s32[6,16]{1,0:T(8,128)} %param.20) | copy-start | bytes 1156
  409.3 10.9 %copy-start.2 = (f32[1,4,12,768]{3,2,1,0:T(8,128)S(1)}, f32[1,4,12,768]{3,2,1,0:T(8,128)}, u32[]{:S(2)}) copy-start(f32[1,4,12,768]{3,2,1,0:T(8,128)} %get-tuple-element.248) | copy-start | bytes 442372
Sparse Core Ops, SparseCore 0:
  275.6 68.7 all-reduce.3
  419.4 219.9 reduce-scatter.2
